TPU v7x, 128 devices: a whole 4x4x4 slice. The times are simulated.
128 devices in a mesh: ctx: 16 (over z_hi, x, core), tp: 8 (over z_lo, y).
Axes of the slice: x: 4, y: 4, z: 4 (z_hi: 2, z_lo: 2; z = z_hi * 2 + z_lo), core: 2. Of those that a mesh axis runs over, the one named last changes fastest.
Arguments:
- query_gate: bfloat16 [32, 1048576], P('tp', 'ctx'), may hold values from -6 to 6
- key_branch: bfloat16 [32, 1048576], P('tp', 'ctx'), may hold values from -6 to 6
- value_branch: bfloat16 [32, 1048576], P('tp', 'ctx'), may hold values from -6 to 6
- long_filter: float32 [32, 1048576], P('tp', 'ctx'), may hold values from -0.005859375 to 0.005859375
- skip_gain: float32 [32], P('tp'), may hold values from 0.5 to 1.5
- out_weight: bfloat16 [32, 32], replicated, may hold values from -1 to 1
Outputs:
- mixed: bfloat16 [32, 1048576], P('tp', 'ctx')
All inputs are finite; a program needn't handle non-finite values.
Results may differ from a plain program's by a relative error of at most 0.02.
Values may be sent and summed in bfloat16 or wider, within the bound.
A program may use at most 256 MiB of HBM per device.

v0:
```python
import math
import jax
import jax.numpy as jnp
from jax import lax
from jax.sharding import PartitionSpec as P

FACTOR = 128


def turn_table(left_idx, right_idx, length, sign):
    phase = left_idx[:, None] * right_idx[None, :] % length
    angle = sign * 2.0 * math.pi / length * phase.astype(jnp.float32)
    return (jnp.cos(angle), jnp.sin(angle))


def apply_form(form, table, values):
    return jnp.einsum(form, table, values, precision=lax.Precision.HIGHEST)


def apply_complex(form, tab_re, tab_im, val_re, val_im, table_first):
    if table_first:
        out_re = apply_form(form, tab_re, val_re) - apply_form(form, tab_im, val_im)
        out_im = apply_form(form, tab_re, val_im) + apply_form(form, tab_im, val_re)
    else:
        out_re = apply_form(form, val_re, tab_re) - apply_form(form, val_im, tab_im)
        out_im = apply_form(form, val_im, tab_re) + apply_form(form, val_re, tab_im)
    return (out_re, out_im)


def times_table(val_re, val_im, tab_re, tab_im):
    return (val_re * tab_re - val_im * tab_im, val_re * tab_im + val_im * tab_re)


def local_forward(val_re, val_im, width_a, width_b):
    iota_a = jnp.arange(width_a, dtype=jnp.int32)
    iota_b = jnp.arange(width_b, dtype=jnp.int32)
    fb_re, fb_im = turn_table(iota_b, iota_b, width_b, -1.0)
    step_re, step_im = apply_complex("cb,...ba->...ca", fb_re, fb_im, val_re, val_im, True)
    tw_re, tw_im = turn_table(iota_b, iota_a, width_a * width_b, -1.0)
    step_re, step_im = times_table(step_re, step_im, tw_re, tw_im)
    fa_re, fa_im = turn_table(iota_a, iota_a, width_a, -1.0)
    return apply_complex("...ca,ad->...cd", fa_re, fa_im, step_re, step_im, False)


def local_inverse(val_re, val_im, width_a, width_b):
    iota_a = jnp.arange(width_a, dtype=jnp.int32)
    iota_b = jnp.arange(width_b, dtype=jnp.int32)
    fa_re, fa_im = turn_table(iota_a, iota_a, width_a, 1.0)
    step_re, step_im = apply_complex("...cd,da->...ca", fa_re, fa_im, val_re, val_im, False)
    tw_re, tw_im = turn_table(iota_b, iota_a, width_a * width_b, 1.0)
    step_re, step_im = times_table(step_re, step_im, tw_re, tw_im)
    fb_re, fb_im = turn_table(iota_b, iota_b, width_b, 1.0)
    return apply_complex("bc,...ca->...ba", fb_re, fb_im, step_re, step_im, True)


def local(query_gate, key_branch, value_branch, long_filter, skip_gain, out_weight):
    ctx_count = lax.axis_size("ctx")
    ctx_index = lax.axis_index("ctx")
    chans, tok_count = query_gate.shape
    width_a = FACTOR
    width_b = tok_count // FACTOR
    residues = 2 * ctx_count
    fft_length = residues * tok_count
    signal = key_branch.astype(jnp.float32) * value_branch.astype(jnp.float32)
    stacked = jnp.concatenate([signal, long_filter], 0)[:, None, :]
    blocks = lax.all_to_all(
        stacked.astype(jnp.bfloat16), "ctx", split_axis=2, concat_axis=1, tiled=True
    ).astype(stacked.dtype)
    dev_idx = jnp.arange(ctx_count, dtype=jnp.int32)
    second_res = jnp.where(dev_idx == 0, ctx_count, residues - dev_idx)
    res_order = jnp.stack([dev_idx, second_res], 1).reshape(residues)
    blk_idx = jnp.arange(ctx_count, dtype=jnp.int32)
    cross_re, cross_im = turn_table(res_order, blk_idx, residues, -1.0)
    spec_re = apply_form("kn,snm->skm", cross_re, blocks)
    spec_im = apply_form("kn,snm->skm", cross_im, blocks)
    spec_re, spec_im = (
        lax.all_to_all(
            spec_re.astype(jnp.bfloat16), "ctx", split_axis=1, concat_axis=2, tiled=True
        ).astype(spec_re.dtype),
        lax.all_to_all(
            spec_im.astype(jnp.bfloat16), "ctx", split_axis=1, concat_axis=2, tiled=True
        ).astype(spec_im.dtype),
    )
    own_res = jnp.stack([ctx_index, jnp.where(ctx_index == 0, ctx_count, residues - ctx_index)])
    offsets = jnp.arange(tok_count, dtype=jnp.int32)
    tw_re, tw_im = turn_table(own_res, offsets, fft_length, -1.0)
    spec_re, spec_im = times_table(spec_re, spec_im, tw_re, tw_im)
    series = spec_re.shape[0]
    spec_re = spec_re.reshape(series, 2, width_b, width_a)
    spec_im = spec_im.reshape(series, 2, width_b, width_a)
    spec_re, spec_im = local_forward(spec_re, spec_im, width_a, width_b)
    sig_re, sig_im = (spec_re[:chans], spec_im[:chans])
    fil_re, fil_im = (spec_re[chans:], spec_im[chans:])
    prod_re, prod_im = times_table(sig_re, sig_im, fil_re, fil_im)
    back_re, back_im = local_inverse(prod_re, prod_im, width_a, width_b)
    back_re = back_re.reshape(chans, 2, tok_count)
    back_im = back_im.reshape(chans, 2, tok_count)
    inv_re, inv_im = turn_table(own_res, offsets, fft_length, 1.0)
    back_re, back_im = times_table(back_re, back_im, inv_re, inv_im)
    back_re = back_re * (1.0 / fft_length)
    back_im = back_im * (1.0 / fft_length)
    block_rows = jnp.arange(1 * lax.axis_size("ctx"), dtype=jnp.int32)
    row_re, row_im = turn_table(block_rows, own_res, residues, 1.0)
    conv = lax.psum_scatter(
        (
            apply_form("nj,cjm->ncm", row_re, back_re) - apply_form("nj,cjm->ncm", row_im, back_im)
        ).astype(jnp.bfloat16),
        "ctx",
        scatter_dimension=0,
        tiled=True,
    ).astype(jnp.float32)[0]
    gated = (query_gate.astype(jnp.float32) * (conv + skip_gain[:, None] * signal)).astype(
        jnp.bfloat16
    )
    tp_index = lax.axis_index("tp")
    out_dev = out_weight.shape[1] // lax.axis_size("tp")
    own_cols = lax.dynamic_slice_in_dim(out_weight, tp_index * out_dev, out_dev, 1)
    mixed = jnp.dot(
        own_cols.T,
        lax.all_gather(gated, "tp", axis=0, tiled=True),
        preferred_element_type=jnp.float32,
    )
    return mixed.astype(jnp.bfloat16)


def solution(mesh):
    placed = (P("tp", "ctx"), P("tp", "ctx"), P("tp", "ctx"), P("tp", "ctx"), P("tp"), P())
    return jax.shard_map(
        local, mesh=mesh, in_specs=placed, out_specs=P("tp", "ctx"), check_vma=False
    )
```

profile of v0, /device:TPU:1, one launch (start us, length us, event | category | flops | bytes accessed | tf_op | source)
XLA Modules:
  0.0 1102.9 jit_solution(4058956443266954925)
XLA Ops:
  6.5 2.0 fusion.52
  8.5 0.5 pad_maximum_fusion
  9.1 49.8 %copy.64 = bf16[8,1,65536]{0,1,2:T(2,128)(2,1)} copy(bf16[8,1,65536]{2,0,1:T(8,128)(2,1)S(1)} %pad_maximum_fusion) | data formatting | bytes 2097152 | tf_op jit(solution)/shard_map/concatenate | solution.py:65
  58.9 0.5 broadcast.406
  59.4 355.8 %reduce = bf16[65536,8]{1,0:T(8,128)(2,1)} reduce(bf16[65536,1,8]{2,1,0:T(2,128)(2,1)} %bitcast.149, bf16[]{:T(256)} %broadcast.406), dimensions={1}, to_apply=%bitcast.134.reduce_sub_computation | reduce | bytes 2097154
  415.2 20.6 %reshape.239 = bf16[16,2,16384]{2,1,0:T(2,128)(2,1)} reshape(bf16[65536,8]{1,0:T(8,128)(2,1)} %reduce) | data formatting | bytes 2097152
  435.8 9.4 all-to-all-start
  445.3 0.1 copy.66
  445.3 0.1 mul.566
  445.4 17.1 %all-to-all-done = bf16[16,2,16384]{2,1,0:T(2,128)(2,1)S(1)} async-done(((bf16[16,2,16384]{2,1,0:T(2,128)(2,1)}), bf16[16,2,16384]{2,1,0:T(2,128)(2,1)S(1)}, u32[]{:S(2)}, u32[]{:S(2)}) %all-to-all-start) | async-done | bytes 1048608 | tf_op jit(solution)/shard_map/all_to_all | solution.py:66
  462.5 39.4 %reshape.240 = bf16[65536,1,8]{2,1,0:T(2,128)(2,1)} reshape(bf16[16,2,16384]{2,1,0:T(2,128)(2,1)S(1)} %all-to-all-done) | data formatting | bytes 2097152
  501.9 58.6 %copy.65 = bf16[8,1,65536]{2,0,1:T(8,128)(2,1)S(1)} copy(bf16[8,1,65536]{0,1,2:T(2,128)(2,1)} %bitcast.150) | data formatting | bytes 2097152 | tf_op jit(solution)/shard_map/all_to_all | solution.py:66
  560.5 2.0 fusion.2
  562.5 2.5 copy.69
  565.0 4.2 all-to-all-start.2
  569.2 0.1 pad_add_fusion.1
  569.3 2.0 fusion.1
  571.3 2.6 copy.67
  573.9 24.0 %all-to-all-done.2 = bf16[8,32,4096]{2,0,1:T(8,128)(2,1)S(1)} async-done(((bf16[8,32,4096]{2,0,1:T(8,128)(2,1)}), bf16[8,32,4096]{2,0,1:T(8,128)(2,1)S(1)}, u32[]{:S(2)}, u32[]{:S(2)}) %all-to-all-start.2) | async-done | bytes 2097184 | tf_op jit(solution)/shard_map/all_to_all | solution.py:80
  597.9 5.5 all-to-all-start.1
  603.4 0.2 all-reduce.3.cloned.1.call-start
  603.7 8.9 fusion.77
  612.5 1.0 multiply_sine_fusion.6
  613.5 0.9 copy.80
  614.4 1.0 multiply_cosine_fusion.6
  615.3 0.8 copy.79
  616.2 1.7 multiply_sine_fusion.7
  617.9 2.1 fusion.81
  620.0 4.8 copy.119
  624.9 4.9 reshape.220
  629.7 2.4 all-to-all-done.1
  632.1 4.8 copy.120
  636.9 5.3 reshape.219
  642.2 21.0 %fusion.34 = f32[8,2,128,512]{3,2,1,0:T(8,128)S(1)} fusion(f32[8,2,512,128]{3,2,1,0:T(8,128)} %reshape.220, f32[8,2,512,128]{3,2,1,0:T(8,128)} %reshape.219, f32[2,512,128]{2,1,0:T(8,128)S(1)} %get-tuple-element.8, f32[2,512,128]{2,1,0:T(8,128)S(1)} %get-tuple-element.7), kind=kOutput, calls=%fused_computation.61 | convolution fusion | flops 6449266688 | bytes 13631488 | tf_op jit(solution)/shard_map/cb,...ba->...ca/dot_general | solution.py:17
  663.3 17.3 %fusion.36 = f32[8,2,128,512]{3,2,1,0:T(8,128)S(1)} fusion(f32[8,2,512,128]{3,2,1,0:T(8,128)S(1)} %copy-done.1, f32[8,2,512,128]{3,2,1,0:T(8,128)S(1)} %copy-done.2, f32[2,512,128]{2,1,0:T(8,128)S(1)} %get-tuple-element.8, f32[2,512,128]{2,1,0:T(8,128)S(1)} %get-tuple-element.7), kind=kOutput, calls=%fused_computation.63 | convolution fusion | flops 6449266688 | bytes 13631488 | tf_op jit(solution)/shard_map/cb,...ba->...ca/dot_general | solution.py:17
  680.5 17.7 %convolution_add_fusion.1 = f32[8,2,128,512]{3,2,1,0:T(8,128)S(1)} fusion(f32[8,2,128,512]{3,2,1,0:T(8,128)S(1)} %fusion.34, f32[8,2,512,128]{3,2,1,0:T(8,128)S(1)} %copy-done.1, f32[8,2,512,128]{3,2,1,0:T(8,128)S(1)} %copy-done.2, f32[2,512,128]{2,1,0:T(8,128)S(1)} %get-tuple-element.8, f32[2,512,128]{2,1,0:T(8,128)S(1)} %get-tuple-element.7), kind=kOutput, calls=%fused_computation.19 | convolution fusion | flops 6450315264 | bytes 17825792 | tf_op jit(solution)/shard_map/cb,...ba->...ca/dot_general | solution.py:17
  698.2 17.3 %convolution_subtract_fusion.2 = f32[8,2,128,512]{3,2,1,0:T(8,128)S(1)} fusion(f32[8,2,128,512]{3,2,1,0:T(8,128)S(1)} %fusion.36, f32[8,2,512,128]{3,2,1,0:T(8,128)S(1)} %copy-done.1, f32[8,2,512,128]{3,2,1,0:T(8,128)S(1)} %copy-done.2, f32[2,512,128]{2,1,0:T(8,128)S(1)} %get-tuple-element.8, f32[2,512,128]{2,1,0:T(8,128)S(1)} %get-tuple-element.7), kind=kOutput, calls=%fused_computation.20 | convolution fusion | flops 6450315264 | bytes 17825792 | tf_op jit(solution)/shard_map/cb,...ba->...ca/dot_general | solution.py:17
  715.6 7.6 fusion.14
  723.2 7.4 fusion.18
  730.6 7.2 convolution_add_fusion
  737.8 7.4 convolution_subtract_fusion.1
  745.3 0.5 multiply_subtract_fusion.2
  745.8 2.1 fusion.87
  747.9 2.1 fusion.89
  750.1 2.1 convolution_add_fusion.2
  752.2 2.5 convolution_subtract_fusion.3
  754.7 10.6 fusion.28
  765.3 11.8 %fusion.30 = f32[4,2,128,512]{3,2,1,0:T(8,128)} fusion(f32[4,2,512,128]{3,2,1,0:T(8,128)S(1)} %convolution_add_fusion.2, f32[4,2,512,128]{3,2,1,0:T(8,128)S(1)} %convolution_subtract_fusion.3, f32[512,128]{1,0:T(8,128)S(1)} %copy-done.8, f32[512,128]{1,0:T(8,128)S(1)} %copy-done.9), kind=kOutput, calls=%fused_computation.57 | convolution fusion | flops 3226468352 | bytes 6815744 | tf_op jit(solution)/shard_map/bc,...ca->...ba/dot_general | solution.py:17
  777.1 12.0 %add_bitcast_fusion = f32[4,2,512,128]{2,3,1,0:T(8,128)} fusion(f32[4,2,128,512]{3,2,1,0:T(8,128)S(1)} %fusion.28, f32[4,2,512,128]{3,2,1,0:T(8,128)S(1)} %convolution_add_fusion.2, f32[4,2,512,128]{3,2,1,0:T(8,128)S(1)} %convolution_subtract_fusion.3, f32[512,128]{1,0:T(8,128)S(1)} %copy-done.8, f32[512,128]{1,0:T(8,128)S(1)} %copy-done.9), kind=kOutput, calls=%fused_computation.29 | convolution fusion | flops 3226992640 | bytes 8912896 | tf_op jit(solution)/shard_map/bc,...ca->...ba/dot_general | solution.py:17
  789.1 3.0 copy.86
  792.1 4.4 reshape.218
  796.5 14.4 %subtract_bitcast_fusion = f32[4,2,512,128]{2,3,1,0:T(8,128)} fusion(f32[4,2,128,512]{3,2,1,0:T(8,128)} %fusion.30, f32[4,2,512,128]{3,2,1,0:T(8,128)S(1)} %convolution_add_fusion.2, f32[4,2,512,128]{3,2,1,0:T(8,128)} %copy-done.3, f32[512,128]{1,0:T(8,128)S(1)} %copy-done.8, f32[512,128]{1,0:T(8,128)} %copy.79), kind=kOutput, calls=%fused_computation.31 | convolution fusion | flops 3226992640 | bytes 8912896 | tf_op jit(solution)/shard_map/bc,...ca->...ba/dot_general | solution.py:17
  810.9 3.0 copy.83
  813.9 4.4 reshape.217
  818.3 17.5 %fusion.9 = f32[16,4,65536]{2,0,1:T(8,128)S(1)} fusion(f32[4,2,65536]{2,1,0:T(2,128)S(1)} %copy-done.4, f32[4,2,65536]{2,1,0:T(2,128)} %reshape.217, f32[2,65536]{1,0:T(2,128)S(1)} %get-tuple-element.10, f32[2,65536]{1,0:T(2,128)S(1)} %get-tuple-element.9, s32[2]{0:T(128)S(1)} %pad_add_fusion.1), kind=kOutput, calls=%fused_computation.25 | convolution fusion | flops 102760896 | bytes 22020104 | tf_op jit(solution)/shard_map/nj,cjm->ncm/dot_general | solution.py:17
  835.8 18.1 %fusion = bf16[16,4,65536]{2,0,1:T(8,128)(2,1)S(1)} fusion(f32[16,4,65536]{2,0,1:T(8,128)S(1)} %fusion.9, f32[4,2,65536]{2,1,0:T(2,128)S(1)} %copy-done.4, f32[4,2,65536]{2,1,0:T(2,128)S(1)} %copy-done.5, f32[2,65536]{1,0:T(2,128)S(1)} %get-tuple-element.10, f32[2,65536]{1,0:T(2,128)S(1)} %get-tuple-element.9, s32[2]{0:T(128)S(1)} %pad_add_fusion.1), kind=kOutput, calls=%fused_computation.1 | convolution fusion | flops 111149504 | bytes 30408712 | tf_op jit(solution)/shard_map/nj,cjm->ncm/dot_general | solution.py:17
  853.9 13.0 %copy.87 = bf16[16,4,65536]{2,1,0:T(4,128)(2,1)} copy(bf16[16,4,65536]{2,0,1:T(8,128)(2,1)S(1)} %fusion) | data formatting | bytes 16777216 | tf_op jit(solution)/shard_map/convert_element_type | solution.py:107
  867.0 0.6 copy-done.14
  867.5 0.7 dynamic-slice
  868.2 160.8 %all-reduce.3.cloned.1.call-done = bf16[16,4,65536]{2,1,0:T(4,128)(2,1)} async-done(((bf16[16,4,65536]{2,1,0:T(4,128)(2,1)}), bf16[16,4,65536]{2,1,0:T(4,128)(2,1)}) %all-reduce.3.cloned.1.call-update) | async-done | bytes 8388624
  1029.0 3.3 fusion.56
  1032.4 54.5 %all-gather.3.cloned.1.call-done = bf16[8,4,65536]{2,1,0:T(4,128)(2,1)} async-done(((bf16[1,4,65536]{2,1,0:T(4,128)(2,1)}), bf16[8,4,65536]{2,1,0:T(4,128)(2,1)}) %all-gather.3.cloned.1.call-update) | async-done | bytes 4194320 | tf_op jit(solution)/shard_map/all_gather | solution.py:120
  1086.8 5.2 reshape.225
  1092.0 3.8 convolution_convert_fusion
  (36 shorter events, 0.2 us)
Async XLA Ops:
  6.5 1085.5 %copy-start = (bf16[32,32]{1,0:T(8,128)(2,1)S(1)}, bf16[32,32]{1,0:T(8,128)(2,1)}, u32[]{:S(2)}) copy-start(bf16[32,32]{1,0:T(8,128)(2,1)} %param.11) | copy-start | bytes 6148
  435.8 26.7 %all-to-all-start = ((bf16[16,2,16384]{2,1,0:T(2,128)(2,1)}), bf16[16,2,16384]{2,1,0:T(2,128)(2,1)S(1)}, u32[]{:S(2)}, u32[]{:S(2)}) async-start(bf16[16,2,16384]{2,1,0:T(2,128)(2,1)} %reshape.239), calls=%async_computation | async-start | bytes 2097152 | tf_op jit(solution)/shard_map/all_to_all | solution.py:66
  565.0 32.9 %all-to-all-start.2 = ((bf16[8,32,4096]{2,0,1:T(8,128)(2,1)}), bf16[8,32,4096]{2,0,1:T(8,128)(2,1)S(1)}, u32[]{:S(2)}, u32[]{:S(2)}) async-start(bf16[8,32,4096]{2,0,1:T(8,128)(2,1)} %copy.69), calls=%async_computation.2 | async-start | bytes 4194304 | tf_op jit(solution)/shard_map/all_to_all | solution.py:80
  597.9 18.3 %copy-start.6 = (bf16[8,32,4096]{2,0,1:T(8,128)(2,1)}, bf16[8,32,4096]{2,0,1:T(8,128)(2,1)S(1)}, u32[]{:S(2)}) copy-start(bf16[8,32,4096]{2,0,1:T(8,128)(2,1)S(1)} %all-to-all-done.2) | copy-start | bytes 6291460
  597.9 34.2 %all-to-all-start.1 = ((bf16[8,32,4096]{2,0,1:T(8,128)(2,1)}), bf16[8,32,4096]{2,0,1:T(8,128)(2,1)}, u32[]{:S(2)}, u32[]{:S(2)}) async-start(bf16[8,32,4096]{2,0,1:T(8,128)(2,1)} %copy.67), calls=%async_computation.1 | async-start | bytes 4194304 | tf_op jit(solution)/shard_map/all_to_all | solution.py:77
  603.4 425.6 %all-reduce.3.cloned.1.call-start = ((), (), s32[]{:S(2)}) async-start(), calls=%async_computation.4 | async-start | bytes 16777216
  642.2 21.0 %copy-start.1 = (f32[8,2,512,128]{3,2,1,0:T(8,128)S(1)}, f32[8,2,512,128]{3,2,1,0:T(8,128)}, u32[]{:S(2)}) copy-start(f32[8,2,512,128]{3,2,1,0:T(8,128)} %reshape.220) | copy-start | bytes 12582916
  642.2 21.0 %copy-start.2 = (f32[8,2,512,128]{3,2,1,0:T(8,128)S(1)}, f32[8,2,512,128]{3,2,1,0:T(8,128)}, u32[]{:S(2)}) copy-start(f32[8,2,512,128]{3,2,1,0:T(8,128)} %reshape.219) | copy-start | bytes 12582916
  698.2 17.4 %copy-start.7 = (f32[512,128]{0,1:T(8,128)S(1)}, f32[512,128]{0,1:T(8,128)}, u32[]{:S(2)}) copy-start(f32[512,128]{0,1:T(8,128)} %get-tuple-element.14) | copy-start | bytes 786436
  752.2 2.5 copy-start.8
  752.2 2.5 copy-start.9
  754.7 22.4 %copy-start.3 = (f32[4,2,512,128]{3,2,1,0:T(8,128)}, f32[4,2,512,128]{3,2,1,0:T(8,128)S(1)}, u32[]{:S(2)}) copy-start(f32[4,2,512,128]{3,2,1,0:T(8,128)S(1)} %convolution_subtract_fusion.3) | copy-start | bytes 6291460
  810.9 7.4 copy-start.4
  818.3 17.5 %copy-start.5 = (f32[4,2,65536]{2,1,0:T(2,128)S(1)}, f32[4,2,65536]{2,1,0:T(2,128)}, u32[]{:S(2)}) copy-start(f32[4,2,65536]{2,1,0:T(2,128)} %reshape.217) | copy-start | bytes 6291460
  866.9 0.7 copy-start.14
  866.9 162.1 %copy-start.10 = (bf16[4,65536]{1,0:T(4,128)(2,1)S(1)}, bf16[4,65536]{1,0:T(4,128)(2,1)}, u32[]{:S(2)}) copy-start(bf16[4,65536]{1,0:T(4,128)(2,1)} %param.8) | copy-start | bytes 1572868
  866.9 162.1 %copy-start.11 = (bf16[4,65536]{1,0:T(4,128)(2,1)S(1)}, bf16[4,65536]{1,0:T(4,128)(2,1)}, u32[]{:S(2)}) copy-start(bf16[4,65536]{1,0:T(4,128)(2,1)} %param.7) | copy-start | bytes 1572868
  866.9 162.1 %copy-start.12 = (bf16[4,65536]{1,0:T(4,128)(2,1)S(1)}, bf16[4,65536]{1,0:T(4,128)(2,1)}, u32[]{:S(2)}) copy-start(bf16[4,65536]{1,0:T(4,128)(2,1)} %param.6) | copy-start | bytes 1572868
  866.9 162.1 %copy-start.13 = (f32[4]{0:T(128)S(1)}, f32[4]{0:T(128)}, u32[]{:S(2)}) copy-start(f32[4]{0:T(128)} %param.10) | copy-start | bytes 52
  866.9 219.9 %all-gather.3.cloned.1.call-start = ((), (), s32[]{:S(2)}) async-start(), calls=%async_computation.3 | async-start | bytes 4718592 | tf_op jit(solution)/shard_map/all_gather | solution.py:120
Sparse Core Ops, SparseCore 0:
  867.0 161.9 all-reduce.2
  1032.5 54.2 all-gather.2
where the time goes:
time: 1110 us; the launch traced here: 1100 us
  other arithmetic  377 us (34%)
  waiting for transfers between devices  259 us (23%)
  local copies, waits for them, and re-layouts  230 us (21%)
  matrix products  204 us (18%)
  starting transfers between devices  19.4 us (2%)
  between operations  14 us (1%)
    unnamed x2, other arithmetic  359 us
    dot_general x20, matrix products, apply_form(): return jnp.einsum(form, table, values, precision=lax.Precision.HIGHEST)  200 us
    unnamed x3, waiting for transfers between devices  161 us
    unnamed x35, local copies, waits for them, and re-layouts  67 us
    all_to_all x1, local copies, waits for them, and re-layouts, local(): lax.all_to_all(stacked.astype(jnp.bfloat16), 'ctx', split_axis=2, concat_...  58.6 us
    all_gather x1, waiting for transfers between devices, local(): lax.all_gather(gated, 'tp', axis=0, tiled=True)  54.5 us
    concatenate x1, local copies, waits for them, and re-layouts, local(): stacked = jnp.concatenate([signal, long_filter], 0)[:, None, :]  49.8 us
    all_to_all x1, waiting for transfers between devices, local(): lax.all_to_all(spec_im.astype(jnp.bfloat16), 'ctx', split_axis=1, concat_...  24 us
  transfers between devices with their start and end apart: 5, of which 5 were waited for; matrix products, arithmetic and copies ran while one was open for 3% of the time, Pallas kernels for 0%

commit v1 on v0

--- a/solution.py
+++ b/solution.py
@@ -63,8 +63,14 @@
     fft_length = residues * tok_count
     signal = key_branch.astype(jnp.float32) * value_branch.astype(jnp.float32)
     stacked = jnp.concatenate([signal, long_filter], 0)[:, None, :]
-    blocks = lax.all_to_all(
-        stacked.astype(jnp.bfloat16), "ctx", split_axis=2, concat_axis=1, tiled=True
+    blocks = jnp.concatenate(
+        lax.all_to_all(
+            jnp.stack(jnp.split(stacked.astype(jnp.bfloat16), lax.axis_size("ctx"), axis=2)),
+            "ctx",
+            0,
+            0,
+        ),
+        axis=1,
     ).astype(stacked.dtype)
     dev_idx = jnp.arange(ctx_count, dtype=jnp.int32)
     second_res = jnp.where(dev_idx == 0, ctx_count, residues - dev_idx)

time: 1110 us -> 595 us (0.54)
  other arithmetic: 377 us -> 31 us
  local copies, waits for them, and re-layouts: 230 us -> 60.7 us
    unnamed x2 -> x16, other arithmetic: 359 us -> 13.1 us
    unnamed x35 -> x32, local copies, waits for them, and re-layouts: 67 us -> 6.44 us
    all_to_all x1 -> x0, local copies, waits for them, and re-layouts: 58.6 us -> none  [local(): lax.all_to_all(stacked.astype(jnp.bfloat16), 'ctx', split_axis=2, concat_...]
    concatenate x1 -> x0, local copies, waits for them, and re-layouts: 49.8 us -> none  [local(): stacked = jnp.concatenate([signal, long_filter], 0)[:, None, :]]
    all_to_all x1, waiting for transfers between devices: 24 us -> 2.04 us  [local(): lax.all_to_all(spec_im.astype(jnp.bfloat16), 'ctx', split_axis=1, concat_...]
    all_to_all x1, waiting for transfers between devices: 2.35 us -> 24.1 us  [local(): lax.all_to_all(spec_re.astype(jnp.bfloat16), 'ctx', split_axis=1, concat_...]
  transfers between devices with their start and end apart: 5 -> 5, of which waited for: 5 -> 5; matrix products, arithmetic and copies ran while one was open for 3% -> 5% of each run, Pallas kernels for 0% -> 0%
where the time goes in v1:
time: 595 us; the launch traced here: 588 us
  waiting for transfers between devices  259 us (44%)
  matrix products  204 us (34%)
  local copies, waits for them, and re-layouts  60.7 us (10%)
  other arithmetic  31 us (5%)
  starting transfers between devices  19.4 us (3%)
  between operations  14 us (2%)
    dot_general x20, matrix products, apply_form(): return jnp.einsum(form, table, values, precision=lax.Precision.HIGHEST)  200 us
    unnamed x3, waiting for transfers between devices  161 us
    all_gather x1, waiting for transfers between devices, local(): lax.all_gather(gated, 'tp', axis=0, tiled=True)  54.5 us
    all_to_all x1, waiting for transfers between devices, local(): lax.all_to_all(spec_re.astype(jnp.bfloat16), 'ctx', split_axis=1, concat_...  24.1 us
    convert_element_type x4, local copies, waits for them, and re-layouts, local(): spec_re, spec_im = (lax.all_to_all(spec_re.astype(jnp.bfloat16), 'ctx', s...  19.6 us
    all_to_all x1, waiting for transfers between devices, local(): lax.all_to_all(jnp.stack(jnp.split(stacked.astype(jnp.bfloat16), lax.axis...  17.2 us
    unnamed x16, other arithmetic  13.1 us
    convert_element_type x1, local copies, waits for them, and re-layouts, local(): conv = lax.psum_scatter((apply_form('nj,cjm->ncm', row_re, back_re) - app...  13 us
  transfers between devices with their start and end apart: 5, of which 5 were waited for; matrix products, arithmetic and copies ran while one was open for 5% of the time, Pallas kernels for 0%

profile of v1, /device:TPU:1, one launch (start us, length us, event | category | flops | bytes accessed | tf_op | source)
XLA Modules:
  0.0 587.9 jit_solution(5155563742916087325)
XLA Ops:
  6.5 2.0 fusion.52
  8.5 0.7 bitcast_dynamic-update-slice_fusion.14
  9.2 0.7 bitcast_dynamic-update-slice_fusion.13
  9.9 0.7 bitcast_dynamic-update-slice_fusion.12
  10.5 0.7 bitcast_dynamic-update-slice_fusion.11
  11.8 0.7 bitcast_dynamic-update-slice_fusion.9
  12.5 0.7 bitcast_dynamic-update-slice_fusion.8
  13.1 0.7 bitcast_dynamic-update-slice_fusion.7
  14.4 0.7 bitcast_dynamic-update-slice_fusion.5
  15.1 0.7 bitcast_dynamic-update-slice_fusion.4
  15.8 0.7 bitcast_dynamic-update-slice_fusion.3
  16.4 0.7 bitcast_dynamic-update-slice_fusion.2
  17.1 0.7 bitcast_dynamic-update-slice_fusion.1
  17.7 0.7 bitcast_dynamic-update-slice_fusion
  18.4 0.7 fusion.101
  19.1 9.1 %all-to-all-start = ((bf16[16,8,1,4096]{3,1,2,0:T(8,128)(2,1)}), bf16[16,8,1,4096]{3,1,2,0:T(8,128)(2,1)S(1)}, u32[]{:S(2)}, u32[]{:S(2)}) async-start(bf16[16,8,1,4096]{3,1,2,0:T(8,128)(2,1)} %fusion.101), calls=%async_computation | async-start | bytes 2097152 | tf_op jit(solution)/shard_map/all_to_all | solution.py:67
  28.4 17.2 %all-to-all-done = bf16[16,8,1,4096]{3,1,2,0:T(8,128)(2,1)S(1)} async-done(((bf16[16,8,1,4096]{3,1,2,0:T(8,128)(2,1)}), bf16[16,8,1,4096]{3,1,2,0:T(8,128)(2,1)S(1)}, u32[]{:S(2)}, u32[]{:S(2)}) %all-to-all-start) | async-done | bytes 1048608 | tf_op jit(solution)/shard_map/all_to_all | solution.py:67
  45.5 2.0 fusion.1
  47.6 2.5 copy.595
  50.1 4.2 all-to-all-start.1
  54.4 2.0 fusion.2
  56.4 2.5 copy.597
  58.9 24.1 %all-to-all-done.1 = bf16[8,32,4096]{2,0,1:T(8,128)(2,1)S(1)} async-done(((bf16[8,32,4096]{2,0,1:T(8,128)(2,1)}), bf16[8,32,4096]{2,0,1:T(8,128)(2,1)S(1)}, u32[]{:S(2)}, u32[]{:S(2)}) %all-to-all-start.1) | async-done | bytes 2097184 | tf_op jit(solution)/shard_map/all_to_all | solution.py:83
  83.0 5.5 all-to-all-start.2
  89.0 8.9 %fusion.77 = (f32[2,65536]{1,0:T(2,128)S(1)}, f32[2,65536]{1,0:T(2,128)S(1)}) fusion(s32[2]{0:T(128)S(1)} %pad_add_fusion.1), kind=kLoop, calls=%fused_computation.140 | loop fusion | flops 1835008 | bytes 1048584 | tf_op jit(solution)/shard_map/cos | solution.py:13
  97.9 1.0 multiply_cosine_fusion.6
  98.9 0.8 copy.607
  99.7 1.0 multiply_sine_fusion.6
  100.7 0.9 copy.608
  101.6 1.7 multiply_sine_fusion.7
  103.3 2.1 fusion.81
  105.4 4.8 copy.647
  110.2 4.9 reshape.224
  115.1 2.0 all-to-all-done.2
  117.2 4.8 copy.646
  122.0 5.1 reshape.225
  127.1 21.0 %fusion.34 = f32[8,2,128,512]{3,2,1,0:T(8,128)S(1)} fusion(f32[8,2,512,128]{3,2,1,0:T(8,128)} %reshape.225, f32[8,2,512,128]{3,2,1,0:T(8,128)} %reshape.224, f32[2,512,128]{2,1,0:T(8,128)S(1)} %get-tuple-element.8, f32[2,512,128]{2,1,0:T(8,128)S(1)} %get-tuple-element.7), kind=kOutput, calls=%fused_computation.90 | convolution fusion | flops 6449266688 | bytes 13631488 | tf_op jit(solution)/shard_map/cb,...ba->...ca/dot_general | solution.py:17
  148.1 17.5 %fusion.32 = f32[8,2,128,512]{3,2,1,0:T(8,128)S(1)} fusion(f32[8,2,512,128]{3,2,1,0:T(8,128)S(1)} %copy-done.2, f32[8,2,512,128]{3,2,1,0:T(8,128)S(1)} %copy-done.1, f32[2,512,128]{2,1,0:T(8,128)S(1)} %get-tuple-element.8, f32[2,512,128]{2,1,0:T(8,128)S(1)} %get-tuple-element.7), kind=kOutput, calls=%fused_computation.88 | convolution fusion | flops 6449266688 | bytes 13631488 | tf_op jit(solution)/shard_map/cb,...ba->...ca/dot_general | solution.py:17
  165.6 17.5 %convolution_subtract_fusion.2 = f32[8,2,128,512]{3,2,1,0:T(8,128)S(1)} fusion(f32[8,2,128,512]{3,2,1,0:T(8,128)S(1)} %fusion.34, f32[8,2,512,128]{3,2,1,0:T(8,128)S(1)} %copy-done.2, f32[8,2,512,128]{3,2,1,0:T(8,128)S(1)} %copy-done.1, f32[2,512,128]{2,1,0:T(8,128)S(1)} %get-tuple-element.8, f32[2,512,128]{2,1,0:T(8,128)S(1)} %get-tuple-element.7), kind=kOutput, calls=%fused_computation.50 | convolution fusion | flops 6450315264 | bytes 17825792 | tf_op jit(solution)/shard_map/cb,...ba->...ca/dot_general | solution.py:17
  183.1 17.5 %convolution_add_fusion.1 = f32[8,2,128,512]{3,2,1,0:T(8,128)S(1)} fusion(f32[8,2,128,512]{3,2,1,0:T(8,128)S(1)} %fusion.32, f32[8,2,512,128]{3,2,1,0:T(8,128)S(1)} %copy-done.2, f32[8,2,512,128]{3,2,1,0:T(8,128)S(1)} %copy-done.1, f32[2,512,128]{2,1,0:T(8,128)S(1)} %get-tuple-element.8, f32[2,512,128]{2,1,0:T(8,128)S(1)} %get-tuple-element.7), kind=kOutput, calls=%fused_computation.49 | convolution fusion | flops 6450315264 | bytes 17825792 | tf_op jit(solution)/shard_map/cb,...ba->...ca/dot_general | solution.py:17
  200.7 7.4 %fusion.18 = f32[8,2,512,128]{3,2,1,0:T(8,128)S(1)} fusion(f32[8,2,128,512]{3,2,1,0:T(8,128)S(1)} %convolution_add_fusion.1, f32[8,2,128,512]{3,2,1,0:T(8,128)S(1)} %convolution_subtract_fusion.2, f32[512,128]{0,1:T(8,128)S(1)} %get-tuple-element.13, f32[512,128]{0,1:T(8,128)S(1)} %copy-done.7), kind=kOutput, calls=%fused_computation.72 | convolution fusion | flops 1613987840 | bytes 13107200 | tf_op jit(solution)/shard_map/...ca,ad->...cd/dot_general | solution.py:17
  208.1 7.4 %fusion.14 = f32[8,2,512,128]{3,2,1,0:T(8,128)S(1)} fusion(f32[8,2,128,512]{3,2,1,0:T(8,128)S(1)} %convolution_add_fusion.1, f32[8,2,128,512]{3,2,1,0:T(8,128)S(1)} %convolution_subtract_fusion.2, f32[512,128]{0,1:T(8,128)S(1)} %get-tuple-element.13, f32[512,128]{0,1:T(8,128)S(1)} %copy-done.7), kind=kOutput, calls=%fused_computation.71 | convolution fusion | flops 1613987840 | bytes 13107200 | tf_op jit(solution)/shard_map/...ca,ad->...cd/dot_general | solution.py:17
  215.5 7.2 %convolution_subtract_fusion.1 = f32[8,2,512,128]{3,2,1,0:T(8,128)S(1)} fusion(f32[8,2,512,128]{3,2,1,0:T(8,128)S(1)} %fusion.18, f32[8,2,128,512]{3,2,1,0:T(8,128)S(1)} %convolution_add_fusion.1, f32[8,2,128,512]{3,2,1,0:T(8,128)S(1)} %convolution_subtract_fusion.2, f32[512,128]{0,1:T(8,128)S(1)} %get-tuple-element.13, f32[512,128]{0,1:T(8,128)S(1)} %copy-done.7), kind=kOutput, calls=%fused_computation.48 | convolution fusion | flops 1615036416 | bytes 17301504 | tf_op jit(solution)/shard_map/...ca,ad->...cd/dot_general | solution.py:17
  222.7 7.6 %convolution_add_fusion = f32[8,2,512,128]{3,2,1,0:T(8,128)S(1)} fusion(f32[8,2,512,128]{3,2,1,0:T(8,128)S(1)} %fusion.14, f32[8,2,128,512]{3,2,1,0:T(8,128)S(1)} %convolution_add_fusion.1, f32[8,2,128,512]{3,2,1,0:T(8,128)S(1)} %convolution_subtract_fusion.2, f32[512,128]{0,1:T(8,128)S(1)} %get-tuple-element.13, f32[512,128]{0,1:T(8,128)S(1)} %copy-done.7), kind=kOutput, calls=%fused_computation.47 | convolution fusion | flops 1615036416 | bytes 17301504 | tf_op jit(solution)/shard_map/...ca,ad->...cd/dot_general | solution.py:17
  230.8 2.1 fusion.106
  233.0 2.1 fusion.104
  235.1 2.1 convolution_subtract_fusion.3
  237.3 2.3 convolution_add_fusion.2
  239.6 10.6 %fusion.28 = f32[4,2,128,512]{3,2,1,0:T(8,128)S(1)} fusion(f32[4,2,512,128]{3,2,1,0:T(8,128)S(1)} %convolution_add_fusion.2, f32[4,2,512,128]{3,2,1,0:T(8,128)S(1)} %convolution_subtract_fusion.3, f32[512,128]{1,0:T(8,128)S(1)} %copy-done.9, f32[512,128]{1,0:T(8,128)S(1)} %copy-done.8), kind=kOutput, calls=%fused_computation.84 | convolution fusion | flops 3226468352 | bytes 6815744 | tf_op jit(solution)/shard_map/bc,...ca->...ba/dot_general | solution.py:17
  250.2 11.8 %fusion.26 = f32[4,2,128,512]{3,2,1,0:T(8,128)} fusion(f32[4,2,512,128]{3,2,1,0:T(8,128)S(1)} %convolution_add_fusion.2, f32[4,2,512,128]{3,2,1,0:T(8,128)S(1)} %convolution_subtract_fusion.3, f32[512,128]{1,0:T(8,128)S(1)} %copy-done.9, f32[512,128]{1,0:T(8,128)S(1)} %copy-done.8), kind=kOutput, calls=%fused_computation.82 | convolution fusion | flops 3226468352 | bytes 6815744 | tf_op jit(solution)/shard_map/bc,...ca->...ba/dot_general | solution.py:17
  262.0 12.2 %subtract_bitcast_fusion = f32[4,2,512,128]{2,3,1,0:T(8,128)} fusion(f32[4,2,128,512]{3,2,1,0:T(8,128)S(1)} %fusion.28, f32[4,2,512,128]{3,2,1,0:T(8,128)S(1)} %convolution_add_fusion.2, f32[4,2,512,128]{3,2,1,0:T(8,128)S(1)} %convolution_subtract_fusion.3, f32[512,128]{1,0:T(8,128)S(1)} %copy-done.9, f32[512,128]{1,0:T(8,128)S(1)} %copy-done.8), kind=kOutput, calls=%fused_computation.61 | convolution fusion | flops 3226992640 | bytes 8912896 | tf_op jit(solution)/shard_map/bc,...ca->...ba/dot_general | solution.py:17
  274.2 3.0 copy.611
  277.2 4.4 reshape.222
  281.5 14.2 %add_bitcast_fusion = f32[4,2,512,128]{2,3,1,0:T(8,128)} fusion(f32[4,2,128,512]{3,2,1,0:T(8,128)} %fusion.26, f32[4,2,512,128]{3,2,1,0:T(8,128)} %copy-done.3, f32[4,2,512,128]{3,2,1,0:T(8,128)S(1)} %convolution_subtract_fusion.3, f32[512,128]{1,0:T(8,128)} %copy.608, f32[512,128]{1,0:T(8,128)S(1)} %copy-done.8), kind=kOutput, calls=%fused_computation.59 | convolution fusion | flops 3226992640 | bytes 8912896 | tf_op jit(solution)/shard_map/bc,...ca->...ba/dot_general | solution.py:17
  295.7 3.0 copy.614
  298.7 4.4 reshape.223
  303.1 17.6 %fusion.9 = f32[16,4,65536]{2,0,1:T(8,128)S(1)} fusion(f32[4,2,65536]{2,1,0:T(2,128)} %reshape.223, f32[4,2,65536]{2,1,0:T(2,128)S(1)} %copy-done.4, f32[2,65536]{1,0:T(2,128)S(1)} %get-tuple-element.10, f32[2,65536]{1,0:T(2,128)S(1)} %get-tuple-element.9, s32[2]{0:T(128)S(1)} %pad_add_fusion.1), kind=kOutput, calls=%fused_computation.55 | convolution fusion | flops 102760896 | bytes 22020104 | tf_op jit(solution)/shard_map/nj,cjm->ncm/dot_general | solution.py:17
  320.7 18.1 %fusion = bf16[16,4,65536]{2,0,1:T(8,128)(2,1)S(1)} fusion(f32[16,4,65536]{2,0,1:T(8,128)S(1)} %fusion.9, f32[4,2,65536]{2,1,0:T(2,128)S(1)} %copy-done.5, f32[4,2,65536]{2,1,0:T(2,128)S(1)} %copy-done.4, f32[2,65536]{1,0:T(2,128)S(1)} %get-tuple-element.10, f32[2,65536]{1,0:T(2,128)S(1)} %get-tuple-element.9, s32[2]{0:T(128)S(1)} %pad_add_fusion.1), kind=kOutput, calls=%fused_computation.1 | convolution fusion | flops 111149504 | bytes 30408712 | tf_op jit(solution)/shard_map/nj,cjm->ncm/dot_general | solution.py:17
  338.8 13.0 %copy.615 = bf16[16,4,65536]{2,1,0:T(4,128)(2,1)} copy(bf16[16,4,65536]{2,0,1:T(8,128)(2,1)S(1)} %fusion) | data formatting | bytes 16777216 | tf_op jit(solution)/shard_map/convert_element_type | solution.py:113
  353.1 160.9 %all-reduce.3.cloned.1.call-done = bf16[16,4,65536]{2,1,0:T(4,128)(2,1)} async-done(((bf16[16,4,65536]{2,1,0:T(4,128)(2,1)}), bf16[16,4,65536]{2,1,0:T(4,128)(2,1)}) %all-reduce.3.cloned.1.call-update) | async-done | bytes 8388624
  514.0 3.3 fusion.56
  517.3 54.5 %all-gather.3.cloned.1.call-done = bf16[8,4,65536]{2,1,0:T(4,128)(2,1)} async-done(((bf16[1,4,65536]{2,1,0:T(4,128)(2,1)}), bf16[8,4,65536]{2,1,0:T(4,128)(2,1)}) %all-gather.3.cloned.1.call-update) | async-done | bytes 4194320 | tf_op jit(solution)/shard_map/all_gather | solution.py:126
  571.8 5.2 reshape.230
  577.0 3.8 convolution_convert_fusion
  (45 shorter events, 3.9 us)
Async XLA Ops:
  6.5 570.5 %copy-start = (bf16[32,32]{1,0:T(8,128)(2,1)S(1)}, bf16[32,32]{1,0:T(8,128)(2,1)}, u32[]{:S(2)}) copy-start(bf16[32,32]{1,0:T(8,128)(2,1)} %param.11) | copy-start | bytes 6148
  19.1 26.5 %all-to-all-start = ((bf16[16,8,1,4096]{3,1,2,0:T(8,128)(2,1)}), bf16[16,8,1,4096]{3,1,2,0:T(8,128)(2,1)S(1)}, u32[]{:S(2)}, u32[]{:S(2)}) async-start(bf16[16,8,1,4096]{3,1,2,0:T(8,128)(2,1)} %fusion.101), calls=%async_computation | async-start | bytes 2097152 | tf_op jit(solution)/shard_map/all_to_all | solution.py:67
  50.1 32.9 %all-to-all-start.1 = ((bf16[8,32,4096]{2,0,1:T(8,128)(2,1)}), bf16[8,32,4096]{2,0,1:T(8,128)(2,1)S(1)}, u32[]{:S(2)}, u32[]{:S(2)}) async-start(bf16[8,32,4096]{2,0,1:T(8,128)(2,1)} %copy.595), calls=%async_computation.1 | async-start | bytes 4194304 | tf_op jit(solution)/shard_map/all_to_all | solution.py:83
  83.0 18.6 %copy-start.6 = (bf16[8,32,4096]{2,0,1:T(8,128)(2,1)}, bf16[8,32,4096]{2,0,1:T(8,128)(2,1)S(1)}, u32[]{:S(2)}) copy-start(bf16[8,32,4096]{2,0,1:T(8,128)(2,1)S(1)} %all-to-all-done.1) | copy-start | bytes 6291460
  83.0 34.2 %all-to-all-start.2 = ((bf16[8,32,4096]{2,0,1:T(8,128)(2,1)}), bf16[8,32,4096]{2,0,1:T(8,128)(2,1)}, u32[]{:S(2)}, u32[]{:S(2)}) async-start(bf16[8,32,4096]{2,0,1:T(8,128)(2,1)} %copy.597), calls=%async_computation.2 | async-start | bytes 4194304 | tf_op jit(solution)/shard_map/all_to_all | solution.py:86
  88.5 425.6 %all-reduce.3.cloned.1.call-start = ((), (), s32[]{:S(2)}) async-start(), calls=%async_computation.4 | async-start | bytes 16777216
  127.1 21.1 %copy-start.1 = (f32[8,2,512,128]{3,2,1,0:T(8,128)S(1)}, f32[8,2,512,128]{3,2,1,0:T(8,128)}, u32[]{:S(2)}) copy-start(f32[8,2,512,128]{3,2,1,0:T(8,128)} %reshape.224) | copy-start | bytes 12582916
  127.1 21.1 %copy-start.2 = (f32[8,2,512,128]{3,2,1,0:T(8,128)S(1)}, f32[8,2,512,128]{3,2,1,0:T(8,128)}, u32[]{:S(2)}) copy-start(f32[8,2,512,128]{3,2,1,0:T(8,128)} %reshape.225) | copy-start | bytes 12582916
  183.1 17.6 %copy-start.7 = (f32[512,128]{0,1:T(8,128)S(1)}, f32[512,128]{0,1:T(8,128)}, u32[]{:S(2)}) copy-start(f32[512,128]{0,1:T(8,128)} %get-tuple-element.14) | copy-start | bytes 786436
  237.3 2.3 copy-start.8
  237.3 2.3 copy-start.9
  239.6 22.4 %copy-start.3 = (f32[4,2,512,128]{3,2,1,0:T(8,128)}, f32[4,2,512,128]{3,2,1,0:T(8,128)S(1)}, u32[]{:S(2)}) copy-start(f32[4,2,512,128]{3,2,1,0:T(8,128)S(1)} %convolution_add_fusion.2) | copy-start | bytes 6291460
  295.7 7.5 %copy-start.4 = (f32[4,2,65536]{2,1,0:T(2,128)S(1)}, f32[4,2,65536]{2,1,0:T(2,128)}, u32[]{:S(2)}) copy-start(f32[4,2,65536]{2,1,0:T(2,128)} %reshape.222) | copy-start | bytes 6291460
  303.1 17.6 %copy-start.5 = (f32[4,2,65536]{2,1,0:T(2,128)S(1)}, f32[4,2,65536]{2,1,0:T(2,128)}, u32[]{:S(2)}) copy-start(f32[4,2,65536]{2,1,0:T(2,128)} %reshape.223) | copy-start | bytes 6291460
  351.8 0.7 copy-start.14
  351.9 162.2 %copy-start.10 = (bf16[4,65536]{1,0:T(4,128)(2,1)S(1)}, bf16[4,65536]{1,0:T(4,128)(2,1)}, u32[]{:S(2)}) copy-start(bf16[4,65536]{1,0:T(4,128)(2,1)} %param.8) | copy-start | bytes 1572868
  351.9 162.2 %copy-start.11 = (bf16[4,65536]{1,0:T(4,128)(2,1)S(1)}, bf16[4,65536]{1,0:T(4,128)(2,1)}, u32[]{:S(2)}) copy-start(bf16[4,65536]{1,0:T(4,128)(2,1)} %param.7) | copy-start | bytes 1572868
  351.9 162.2 %copy-start.12 = (bf16[4,65536]{1,0:T(4,128)(2,1)S(1)}, bf16[4,65536]{1,0:T(4,128)(2,1)}, u32[]{:S(2)}) copy-start(bf16[4,65536]{1,0:T(4,128)(2,1)} %param.6) | copy-start | bytes 1572868
  351.9 162.2 %copy-start.13 = (f32[4]{0:T(128)S(1)}, f32[4]{0:T(128)}, u32[]{:S(2)}) copy-start(f32[4]{0:T(128)} %param.10) | copy-start | bytes 52
  351.9 219.9 %all-gather.3.cloned.1.call-start = ((), (), s32[]{:S(2)}) async-start(), calls=%async_computation.3 | async-start | bytes 4718592 | tf_op jit(solution)/shard_map/all_gather | solution.py:126
Sparse Core Ops, SparseCore 0:
  352.0 161.9 all-reduce.2
  517.4 54.2 all-gather.2
